TPU v7x, 256 devices: a whole 4x4x8 slice. The times are simulated.
256 devices in a mesh: front: 8 (over x, core), grp: 32 (over y, z).
Axes of the slice: x: 4, y: 4, z: 8, core: 2. Of those that a mesh axis runs over, the one named last changes fastest.
Arguments:
- panel_block: bfloat16 [8, 4608, 1024], P('front', 'grp'), may hold values from -0.1796875 to 0.1796875
- trailing: float32 [8, 4608, 4608], P('front', 'grp')
- inverse: float32 [8, 1024, 1024], P('front')
- weights: float32 [8, 4608], P('front'), may hold values from -0.09375 to 0.09375
- live_size: int32 [8], P('front'), may hold values from 2304 to 4608, as said below
- column_source: int32 [8, 4608], P('front'), may hold values from 0 to 4607, each once within a row
- destination: int32 [8, 4608, 1], P('front', 'grp'), may hold values from 0 to 7; in each aligned block of 144 rows (0 to 143, 144 to 287, ..., all dimensions but the last counted through in order) at most 36 rows name the same one
- row_offset: int32 [8, 4608], P('front', 'grp'), may hold values from 0 to 143
Outputs:
- factor: float32 [8, 4608, 1024], P('front', 'grp')
- checksum: float32 [8, 4608], P('front', 'grp')
- ancestor: float32 [8, 4608, 4608], P('front', 'grp')
Inputs may be any that keep to these rules, and one draw needn't show every extreme that they name: `live_size`: each front's live size is 4608 minus a multiple of 576; one front is full. `destination`: among the 144 rows of one device at most 36 rows name the same ancestor front. `column_source`: each front's row is a permutation.
All inputs are finite; a program needn't handle non-finite values.
Results may differ from a plain program's by a relative error of at most 0.0003.
Values may be sent and summed in bfloat16 or wider, within the bound.
A program may use at most 128 MiB of HBM per device.

v0:
```python
import jax
import jax.numpy as jnp
from jax import lax
from jax.sharding import PartitionSpec as P


def place_columns(rows, source, live_count):
    keep_cols = (source < live_count).astype(jnp.float32)
    return jnp.take(rows, source, axis=1) * keep_cols[None, :]


def on_device(
    panel_block, trailing, inverse, weights, live_size, column_source, destination, row_offset
):
    highest_precision = lax.Precision.HIGHEST
    row_count = trailing.shape[1]
    col_count = trailing.shape[2]
    fronts = lax.axis_size("front")
    capacity = max(2, 2 * row_count // fronts)
    trail_rows = trailing[0]
    inverse_rows = inverse[0]
    live_count = live_size[0]
    panel_f32 = panel_block[0].astype(jnp.float32)
    factor = jnp.dot(panel_f32, inverse_rows.T, precision=highest_precision)
    update = lax.dot_general(
        factor,
        lax.all_gather(factor, "grp", axis=0, tiled=True),
        (((1,), (1,)), ((), ())),
        precision=highest_precision,
        preferred_element_type=jnp.float32,
    )
    schur_rows = trail_rows - update
    positions = jnp.arange(col_count, dtype=jnp.int32)
    colmask = (positions < live_count).astype(jnp.float32)
    masked_weights = weights[0] * colmask
    checksum = jnp.dot(schur_rows, masked_weights, precision=highest_precision)
    global_rows = lax.axis_index("grp") * row_count + jnp.arange(row_count, dtype=jnp.int32)
    live_rows = global_rows < live_count
    dest_front = destination[0, :, 0]
    front_ids = jnp.arange(fronts, dtype=jnp.int32)
    onehot = ((dest_front[:, None] == front_ids[None, :]) & live_rows[:, None]).astype(jnp.int32)
    running = jnp.cumsum(onehot, axis=0)
    slot_index = jnp.sum(onehot * (running - 1), axis=1)
    dest_live = jnp.where(live_rows, dest_front, fronts)
    row_tags = (
        jnp.full((fronts, capacity), -1.0, jnp.float32)
        .at[dest_live, slot_index]
        .set(row_offset[0].astype(jnp.float32), mode="drop")
    )
    permuted = place_columns(schur_rows, column_source[0], live_count)
    bucket = (
        jnp.zeros((fronts, capacity, col_count), jnp.float32)
        .at[dest_live, slot_index]
        .set(permuted, mode="drop")
    )
    received, received_tags = (
        lax.all_to_all(bucket, "front", split_axis=0, concat_axis=0, tiled=True),
        lax.all_to_all(row_tags, "front", split_axis=0, concat_axis=0, tiled=True),
    )
    flat_rows = received.reshape(fronts * capacity, col_count)
    flat_tags = received_tags.reshape(fronts * capacity)
    target_row = jnp.where(flat_tags < 0.0, row_count, flat_tags.astype(jnp.int32))
    ancestor = (
        jnp.zeros((row_count, col_count), jnp.float32).at[target_row].add(flat_rows, mode="drop")
    )
    return (factor[None], checksum[None], ancestor[None])


def solution(mesh):
    placed = (
        P("front", "grp", None),
        P("front", "grp", None),
        P("front", None, None),
        P("front", None),
        P("front"),
        P("front", None),
        P("front", "grp", None),
        P("front", "grp"),
    )
    return jax.shard_map(
        on_device,
        mesh=mesh,
        in_specs=placed,
        out_specs=(P("front", "grp", None), P("front", "grp"), P("front", "grp", None)),
        check_vma=False,
    )
```

profile of v0, /device:TPU:1, one launch (start us, length us, event | category | flops | bytes accessed | tf_op | source)
XLA Modules:
  0.0 366.7 jit_solution(13603879904250098993)
XLA Ops:
  7.3 0.9 copy-done
  8.1 5.4 %fusion = f32[144,1024]{1,0:T(8,128)} fusion(f32[1,1024,1024]{2,1,0:T(8,128)} %param.10, bf16[1,144,1024]{2,1,0:T(8,128)(2,1)S(1)} %copy-done), kind=kOutput, calls=%fused_computation.6 | convolution fusion | flops 1811939328 | bytes 5079040 | tf_op jit(solution)/shard_map/dot_general | solution.py:24
  14.3 0.6 reduce-window.6
  14.9 0.2 slice_reduce_fusion
  15.1 0.1 add_bitcast_fusion
  15.3 0.6 broadcast_in_dim.49
  15.9 22.1 %scatter_fusion = f32[8,36]{1,0:T(8,128)} fusion(f32[8,36]{1,0:T(8,128)} %broadcast_in_dim.49, s32[144]{0:T(256)S(1)} %bitcast.39, f32[144]{0:T(256)S(1)} %bitcast.45), kind=kCustom, calls=%fused_computation.1 | custom fusion | bytes 2880 | tf_op jit(solution)/shard_map/scatter | solution.py:48
  37.9 6.4 %all-to-all-start = ((f32[8,1,36]{2,1,0:T(1,128)}), f32[8,1,36]{2,1,0:T(1,128)S(1)}, u32[]{:S(2)}, u32[]{:S(2)}) async-start(f32[8,1,36]{2,1,0:T(1,128)} %bitcast.15), calls=%async_computation | async-start | bytes 8192 | tf_op jit(solution)/shard_map/all_to_all | solution.py:58
  44.4 0.1 fusion.6
  44.6 123.4 %all-gather.2.cloned.1.call-done = f32[4608,1024]{1,0:T(8,128)} async-done(((f32[144,1024]{1,0:T(8,128)}), f32[4608,1024]{1,0:T(8,128)}) %all-gather.2.cloned.1.call-update) | async-done | bytes 18874384 | tf_op jit(solution)/shard_map/all_gather | solution.py:27
  168.0 23.8 %convolution_subtract_fusion = f32[144,4608]{1,0:T(8,128)S(1)} fusion(f32[144,1024]{1,0:T(8,128)} %fusion, f32[4608,1024]{1,0:T(8,128)} %all-gather.2.cloned.1.call-done, f32[1,144,4608]{2,1,0:T(8,128)} %param.9), kind=kOutput, calls=%fused_computation.4 | convolution fusion | flops 8154390528 | bytes 24772608 | tf_op jit(solution)/shard_map/dot_general | solution.py:25
  191.8 3.4 copy.17
  195.2 14.1 %gather_fusion = f32[4608,144]{1,0:T(8,128)} fusion(f32[144,4608]{0,1:T(8,128)} %copy.17, s32[5120]{0:T(1024)S(1)} %pad_clamp_fusion), kind=kCustom, calls=%fused_computation | custom fusion | bytes 5326848 | tf_op jit(solution)/shard_map/jit(_take)/gather | solution.py:9
  209.3 6.4 %multiply_bitcast_fusion = f32[144,4608]{0,1:T(8,128)} fusion(f32[4608,144]{1,0:T(8,128)} %gather_fusion, f32[4608]{0:T(1024)S(1)} %fusion.7, pred[4608]{0:T(1024)(128)(4,1)S(1)} %compare_and_fusion), kind=kLoop, calls=%fused_computation.5 | loop fusion | flops 1327104 | bytes 5331456 | tf_op jit(solution)/shard_map/mul | solution.py:9
  215.7 5.3 %copy.18 = f32[144,4608]{1,0:T(8,128)} copy(f32[144,4608]{0,1:T(8,128)} %multiply_bitcast_fusion) | data formatting | bytes 5308416 | tf_op jit(solution)/shard_map/mul | solution.py:9
  221.0 3.0 broadcast_in_dim.53
  224.0 39.0 %scatter_fusion.1 = f32[8,36,4608]{2,0,1:T(8,128)} fusion(f32[8,36,4608]{2,0,1:T(8,128)} %broadcast_in_dim.53, s32[144]{0:T(256)S(1)} %bitcast.40, f32[144,4608]{1,0:T(8,128)} %copy.18), kind=kCustom, calls=%fused_computation.2 | custom fusion | bytes 7963776 | tf_op jit(solution)/shard_map/scatter | solution.py:54
  263.0 8.1 %copy.19 = f32[8,36,4608]{2,1,0:T(8,128)} copy(f32[8,36,4608]{2,0,1:T(8,128)} %scatter_fusion.1) | data formatting | bytes 10616832 | tf_op jit(solution)/shard_map/scatter | solution.py:54
  271.1 5.4 %all-to-all-start.1 = ((f32[8,36,4608]{2,1,0:T(8,128)}), f32[8,36,4608]{2,1,0:T(8,128)}, u32[]{:S(2)}, u32[]{:S(2)}) async-start(f32[8,36,4608]{2,1,0:T(8,128)} %copy.19), calls=%async_computation.1 | async-start | bytes 11796480 | tf_op jit(solution)/shard_map/all_to_all | solution.py:57
  276.7 0.1 select_n.81
  276.8 2.7 fusion.15
  279.5 64.2 %all-to-all-done.1 = f32[8,36,4608]{2,1,0:T(8,128)} async-done(((f32[8,36,4608]{2,1,0:T(8,128)}), f32[8,36,4608]{2,1,0:T(8,128)}, u32[]{:S(2)}, u32[]{:S(2)}) %all-to-all-start.1) | async-done | bytes 5308448 | tf_op jit(solution)/shard_map/all_to_all | solution.py:57
  343.7 5.6 %reshape.169 = f32[288,4608]{1,0:T(8,128)} reshape(f32[8,36,4608]{2,1,0:T(8,128)} %all-to-all-done.1) | data formatting | bytes 10616832 | tf_op jit(solution)/shard_map/reshape | solution.py:60
  349.3 10.6 %scatter_custom_fusion.2 = f32[144,4608]{1,0:T(8,128)} fusion(s32[288]{0:T(512)S(1)} %fusion.13, f32[288,4608]{1,0:T(8,128)} %reshape.169, f32[]{:T(128)} %constant.13.clone.1), kind=kCustom, calls=%fused_computation.8 | custom fusion | flops 1327104 | bytes 2654720 | tf_op jit(solution)/shard_map/scatter-add | solution.py:64
  (31 shorter events, 0.4 us)
Async XLA Ops:
  7.2 1.0 copy-start
  7.2 7.1 %copy-start.4 = (s32[1,144,1]{1,2,0:T(1,128)S(1)}, s32[1,144,1]{1,2,0:T(1,128)}, u32[]{:S(2)}) copy-start(s32[1,144,1]{1,2,0:T(1,128)} %param.14) | copy-start | bytes 1732
  7.2 7.9 %copy-start.5 = (s32[1,144]{1,0:T(1,128)S(1)}, s32[1,144]{1,0:T(1,128)}, u32[]{:S(2)}) copy-start(s32[1,144]{1,0:T(1,128)} %param.15) | copy-start | bytes 1732
  7.2 37.2 %copy-start.2 = (s32[1,4608]{1,0:T(1,128)S(1)}, s32[1,4608]{1,0:T(1,128)}, u32[]{:S(2)}) copy-start(s32[1,4608]{1,0:T(1,128)} %param.13) | copy-start | bytes 55300
  7.2 160.8 %all-gather.2.cloned.1.call-start = ((), (), s32[]{:S(2)}) async-start(), calls=%async_computation.2 | async-start | bytes 19464192 | tf_op jit(solution)/shard_map/all_gather | solution.py:27
  37.9 233.2 %all-to-all-start = ((f32[8,1,36]{2,1,0:T(1,128)}), f32[8,1,36]{2,1,0:T(1,128)S(1)}, u32[]{:S(2)}, u32[]{:S(2)}) async-start(f32[8,1,36]{2,1,0:T(1,128)} %bitcast.15), calls=%async_computation | async-start | bytes 8192 | tf_op jit(solution)/shard_map/all_to_all | solution.py:58
  271.1 5.4 %copy-start.3 = (f32[1,4608]{1,0:T(1,128)S(1)}, f32[1,4608]{1,0:T(1,128)}, u32[]{:S(2)}) copy-start(f32[1,4608]{1,0:T(1,128)} %param.11) | copy-start | bytes 55300
  271.1 72.6 %all-to-all-start.1 = ((f32[8,36,4608]{2,1,0:T(8,128)}), f32[8,36,4608]{2,1,0:T(8,128)}, u32[]{:S(2)}, u32[]{:S(2)}) async-start(f32[8,36,4608]{2,1,0:T(8,128)} %copy.19), calls=%async_computation.1 | async-start | bytes 11796480 | tf_op jit(solution)/shard_map/all_to_all | solution.py:57
  276.8 83.1 %copy-start.1 = (bf16[1,144,1024]{2,1,0:T(8,128)(2,1)S(1)}, bf16[1,144,1024]{2,1,0:T(8,128)(2,1)}, u32[]{:S(2)}) copy-start(bf16[1,144,1024]{2,1,0:T(8,128)(2,1)} %param.8) | copy-start | bytes 884740
Sparse Core Ops, SparseCore 0:
  13.7 154.2 all-gather.1
where the time goes:
time: 368 us; the launch traced here: 367 us
  waiting for transfers between devices  188 us (51%)
  local copies, waits for them, and re-layouts  102 us (28%)
  matrix products  31.9 us (9%)
  other arithmetic  18 us (5%)
  between operations  14.8 us (4%)
  starting transfers between devices  11.9 us (3%)
    all_gather x1, waiting for transfers between devices, on_device(): lax.all_gather(factor, 'grp', axis=0, tiled=True)  123 us
    all_to_all x1, waiting for transfers between devices, on_device(): lax.all_to_all(bucket, 'front', split_axis=0, concat_axis=0, tiled=True)  64.2 us
    scatter x2, local copies, waits for them, and re-layouts, on_device(): bucket = jnp.zeros((fronts, capacity, col_count), jnp.float32).at[dest_li...  47.1 us
    dot_general x1, matrix products, on_device(): lax.dot_general(factor, lax.all_gather(factor, 'grp', axis=0, tiled=True)...  23.8 us
    scatter x1, local copies, waits for them, and re-layouts, on_device(): row_tags = jnp.full((fronts, capacity), -1.0, jnp.float32).at[dest_live,...  22.1 us
    gather x1, local copies, waits for them, and re-layouts, place_columns(): return jnp.take(rows, source, axis=1) * keep_cols[None, :]  14.1 us
    scatter-add x1, other arithmetic, on_device(): jnp.zeros((row_count, col_count), jnp.float32).at[target_row]  10.6 us
  transfers between devices with their start and end apart: 3, of which 2 were waited for; matrix products, arithmetic and copies ran while one was open for 35% of the time, Pallas kernels for 0%

commit v1 on v0

--- a/solution.py
+++ b/solution.py
@@ -2,6 +2,18 @@
 import jax.numpy as jnp
 from jax import lax
 from jax.sharding import PartitionSpec as P
+
+
+def meet_the_zones(raw):
+    return jnp.concatenate(
+        jax.lax.all_to_all(
+            jnp.stack([raw for _ in range(jax.lax.axis_size("grp"))]),
+            axis_name="grp",
+            split_axis=0,
+            concat_axis=0,
+        ),
+        axis=0,
+    )
 
 
 def place_columns(rows, source, live_count):
@@ -24,7 +36,7 @@
     factor = jnp.dot(panel_f32, inverse_rows.T, precision=highest_precision)
     update = lax.dot_general(
         factor,
-        lax.all_gather(factor, "grp", axis=0, tiled=True),
+        meet_the_zones(factor),
         (((1,), (1,)), ((), ())),
         precision=highest_precision,
         preferred_element_type=jnp.float32,

time: 368 us -> 682 us (1.85)
  the two profiles are of different devices: /device:TPU:1 before, /device:TPU:184 now
where the time goes in v1:
time: 682 us; the launch traced here: 680 us
  waiting for transfers between devices  503 us (74%)
  local copies, waits for them, and re-layouts  108 us (16%)
  matrix products  31.1 us (5%)
  starting transfers between devices  18.7 us (3%)
  other arithmetic  18 us (3%)
    all_to_all x1, waiting for transfers between devices, meet_the_zones(): jax.lax.all_to_all(jnp.stack([raw for _ in range(jax.lax.axis_size('grp')...  438 us
    all_to_all x1, waiting for transfers between devices, on_device(): lax.all_to_all(bucket, 'front', split_axis=0, concat_axis=0, tiled=True)  65.1 us
    scatter x2, local copies, waits for them, and re-layouts, on_device(): bucket = jnp.zeros((fronts, capacity, col_count), jnp.float32).at[dest_li...  49.1 us
    dot_general x1, matrix products, on_device(): lax.dot_general(factor, meet_the_zones(factor), (((1,), (1,)), ((), ())),...  23.7 us
    scatter x1, local copies, waits for them, and re-layouts, on_device(): row_tags = jnp.full((fronts, capacity), -1.0, jnp.float32).at[dest_live,...  17 us
    gather x1, local copies, waits for them, and re-layouts, place_columns(): return jnp.take(rows, source, axis=1) * keep_cols[None, :]  14.1 us
  transfers between devices with their start and end apart: 3, of which 2 were waited for; matrix products, arithmetic and copies ran while one was open for 19% of the time, Pallas kernels for 0%

profile of v1, /device:TPU:184, one launch (start us, length us, event | category | flops | bytes accessed | tf_op | source)
XLA Modules:
  0.0 680.1 jit_solution(12196984543663282156)
XLA Ops:
  0.6 1.0 copy-done
  1.6 4.6 fusion
  6.2 8.9 %stack.2 = f32[32,144,1024]{2,1,0:T(8,128)} broadcast(f32[144,1024]{1,0:T(8,128)S(1)} %fusion), dimensions={1,2} | broadcast | bytes 19464192 | tf_op jit(solution)/shard_map/stack | solution.py:10
  15.1 9.5 %all-to-all-start = ((f32[32,144,1024]{2,1,0:T(8,128)}), f32[32,144,1024]{2,1,0:T(8,128)}, u32[]{:S(2)}, u32[]{:S(2)}) async-start(f32[32,144,1024]{2,1,0:T(8,128)} %stack.2), calls=%async_computation | async-start | bytes 37748736 | tf_op jit(solution)/shard_map/all_to_all | solution.py:9
  25.3 0.6 reduce-window.6
  25.9 0.2 slice_reduce_fusion
  26.3 0.6 broadcast_in_dim.49
  26.9 17.0 %scatter_fusion = f32[8,36]{1,0:T(8,128)} fusion(f32[8,36]{1,0:T(8,128)} %broadcast_in_dim.49, s32[144]{0:T(256)S(1)} %bitcast.40, f32[144]{0:T(256)S(1)} %bitcast.46), kind=kCustom, calls=%fused_computation.1 | custom fusion | bytes 2880 | tf_op jit(solution)/shard_map/scatter | solution.py:60
  44.1 437.6 %all-to-all-done = f32[32,144,1024]{2,1,0:T(8,128)} async-done(((f32[32,144,1024]{2,1,0:T(8,128)}), f32[32,144,1024]{2,1,0:T(8,128)}, u32[]{:S(2)}, u32[]{:S(2)}) %all-to-all-start) | async-done | bytes 18874400 | tf_op jit(solution)/shard_map/all_to_all | solution.py:9
  481.7 4.3 all-to-all-start.1
  486.0 23.7 %convolution_subtract_fusion = f32[144,4608]{1,0:T(8,128)S(1)} fusion(f32[144,1024]{1,0:T(8,128)S(1)} %fusion, f32[4608,1024]{1,0:T(8,128)} %bitcast.4, f32[1,144,4608]{2,1,0:T(8,128)} %param.9), kind=kOutput, calls=%fused_computation.4 | convolution fusion | flops 8154390528 | bytes 24772608 | tf_op jit(solution)/shard_map/dot_general | solution.py:37
  509.7 3.4 copy.17
  513.1 14.1 %gather_fusion = f32[4608,144]{1,0:T(8,128)} fusion(f32[144,4608]{0,1:T(8,128)} %copy.17, s32[5120]{0:T(1024)S(1)} %pad_clamp_fusion), kind=kCustom, calls=%fused_computation | custom fusion | bytes 5326848 | tf_op jit(solution)/shard_map/jit(_take)/gather | solution.py:21
  527.2 6.4 multiply_bitcast_fusion
  533.7 5.3 copy.18
  538.9 3.0 broadcast_in_dim.53
  541.9 41.0 %scatter_fusion.1 = f32[8,36,4608]{2,0,1:T(8,128)} fusion(f32[8,36,4608]{2,0,1:T(8,128)} %broadcast_in_dim.53, s32[144]{0:T(256)S(1)} %bitcast.41, f32[144,4608]{1,0:T(8,128)} %copy.18), kind=kCustom, calls=%fused_computation.2 | custom fusion | bytes 7963776 | tf_op jit(solution)/shard_map/scatter | solution.py:66
  582.9 8.1 %copy.19 = f32[8,36,4608]{2,1,0:T(8,128)} copy(f32[8,36,4608]{2,0,1:T(8,128)} %scatter_fusion.1) | data formatting | bytes 10616832 | tf_op jit(solution)/shard_map/scatter | solution.py:66
  591.0 4.9 all-to-all-start.2
  596.1 0.1 select_n.81
  596.2 2.7 fusion.15
  598.9 65.1 %all-to-all-done.2 = f32[8,36,4608]{2,1,0:T(8,128)} async-done(((f32[8,36,4608]{2,1,0:T(8,128)}), f32[8,36,4608]{2,1,0:T(8,128)}, u32[]{:S(2)}, u32[]{:S(2)}) %all-to-all-start.2) | async-done | bytes 5308448 | tf_op jit(solution)/shard_map/all_to_all | solution.py:69
  664.0 5.6 reshape.175
  669.6 10.6 %scatter_custom_fusion.2 = f32[144,4608]{1,0:T(8,128)} fusion(s32[288]{0:T(512)S(1)} %fusion.13, f32[288,4608]{1,0:T(8,128)} %reshape.175, f32[]{:T(128)} %constant.13.clone.1), kind=kCustom, calls=%fused_computation.8 | custom fusion | flops 1327104 | bytes 2654720 | tf_op jit(solution)/shard_map/scatter-add | solution.py:76
  (33 shorter events, 0.5 us)
Async XLA Ops:
  0.6 1.0 copy-start
  6.2 479.8 %copy-start.2 = (f32[144,1024]{1,0:T(8,128)}, f32[144,1024]{1,0:T(8,128)S(1)}, u32[]{:S(2)}) copy-start(f32[144,1024]{1,0:T(8,128)S(1)} %fusion) | copy-start | bytes 1769476
  15.1 10.1 %copy-start.5 = (s32[1,144,1]{1,2,0:T(1,128)S(1)}, s32[1,144,1]{1,2,0:T(1,128)}, u32[]{:S(2)}) copy-start(s32[1,144,1]{1,2,0:T(1,128)} %param.14) | copy-start | bytes 1732
  15.1 11.0 %copy-start.6 = (s32[1,144]{1,0:T(1,128)S(1)}, s32[1,144]{1,0:T(1,128)}, u32[]{:S(2)}) copy-start(s32[1,144]{1,0:T(1,128)} %param.15) | copy-start | bytes 1732
  15.1 11.0 %copy-start.3 = (s32[1,4608]{1,0:T(1,128)S(1)}, s32[1,4608]{1,0:T(1,128)}, u32[]{:S(2)}) copy-start(s32[1,4608]{1,0:T(1,128)} %param.13) | copy-start | bytes 55300
  15.1 466.6 %all-to-all-start = ((f32[32,144,1024]{2,1,0:T(8,128)}), f32[32,144,1024]{2,1,0:T(8,128)}, u32[]{:S(2)}, u32[]{:S(2)}) async-start(f32[32,144,1024]{2,1,0:T(8,128)} %stack.2), calls=%async_computation | async-start | bytes 37748736 | tf_op jit(solution)/shard_map/all_to_all | solution.py:9
  481.7 109.3 %all-to-all-start.1 = ((f32[8,1,36]{2,1,0:T(1,128)}), f32[8,1,36]{2,1,0:T(1,128)S(1)}, u32[]{:S(2)}, u32[]{:S(2)}) async-start(f32[8,1,36]{2,1,0:T(1,128)} %bitcast.16), calls=%async_computation.1 | async-start | bytes 8192 | tf_op jit(solution)/shard_map/all_to_all | solution.py:70
  591.0 4.9 copy-start.4
  591.0 73.0 %all-to-all-start.2 = ((f32[8,36,4608]{2,1,0:T(8,128)}), f32[8,36,4608]{2,1,0:T(8,128)}, u32[]{:S(2)}, u32[]{:S(2)}) async-start(f32[8,36,4608]{2,1,0:T(8,128)} %copy.19), calls=%async_computation.2 | async-start | bytes 11796480 | tf_op jit(solution)/shard_map/all_to_all | solution.py:69
  596.2 83.9 %copy-start.1 = (bf16[1,144,1024]{2,1,0:T(8,128)(2,1)S(1)}, bf16[1,144,1024]{2,1,0:T(8,128)(2,1)}, u32[]{:S(2)}) copy-start(bf16[1,144,1024]{2,1,0:T(8,128)(2,1)} %param.8) | copy-start | bytes 884740
